TPU v7x, 32 devices: a whole 2x2x4 slice. The times are simulated.
32 devices in a mesh: groups: 2 (over y), seq: 4 (over z), head: 2 (over x), rep: 2 (over core).
Axes of the slice: x: 2, y: 2, z: 4, core: 2. Of those that a mesh axis runs over, the one named last changes fastest.
Arguments:
- document_query: bfloat16 [4096, 8192], P(('groups', 'seq', 'rep'), 'head'), parts along dimension 0, may hold values from -6 to 6
- document_key: bfloat16 [4096, 8192], P(('groups', 'seq', 'rep'), 'head'), parts along dimension 0, may hold values from -0.059814453 to 0.059814453
- document_value: bfloat16 [4096, 8192], P(('groups', 'seq', 'rep'), 'head'), parts along dimension 0, may hold values from -6 to 6
- document_decay: float32 [4096, 64], P(('groups', 'seq', 'rep'), 'head'), parts along dimension 0, may hold values from 0 to 1, as said below
- passage_query: bfloat16 [16, 256, 8192], P(('groups', 'seq', 'rep'), None, 'head'), parts along dimension 0, may hold values from -6 to 6
- passage_key: bfloat16 [16, 256, 8192], P(('groups', 'seq', 'rep'), None, 'head'), parts along dimension 0, may hold values from -0.059814453 to 0.059814453
- passage_value: bfloat16 [16, 256, 8192], P(('groups', 'seq', 'rep'), None, 'head'), parts along dimension 0, may hold values from -6 to 6
- passage_gate: bfloat16 [16, 256, 8192], P(('groups', 'seq', 'rep'), None, 'head'), parts along dimension 0, may hold values from -8 to 8
- passage_decay: float32 [16, 256, 64], P(('groups', 'seq', 'rep'), None, 'head'), parts along dimension 0, may hold values from 0 to 1, as said below
- passage_length: int32 [16], P(('groups', 'seq', 'rep')), parts along dimension 0, may hold values from 64 to 256, as said below
- norm_gain: float32 [8192], P('head'), may hold values from 0.1 to 1.9
Outputs:
- document_output: bfloat16 [4096, 8192], P(('groups', 'seq', 'rep'), 'head'), parts along dimension 0
- passage_output: bfloat16 [16, 256, 8192], P(('groups', 'seq', 'rep'), None, 'head'), parts along dimension 0
There are 2 independent parts, one for each index of `groups`. A program takes and returns all parts, laid end to end along the dimension named above; an argument that names none is the same for every part. Nothing has to cross between parts.
Inputs may be any that keep to these rules, and one draw needn't show every extreme that they name: `document_decay`: positive per-position log-decay rates. `passage_decay`: positive per-position log-decay rates. `passage_length`: a passage's valid tokens are its first ones.
All inputs are finite; a program needn't handle non-finite values.
Results may differ from a plain program's by a relative error of at most 0.0046.
Values sent between devices are 32-bit elements; how exact they have to be, the bound alone decides.
A program may use at most 128 MiB of HBM per device.

v0:
```python
import jax
import jax.numpy as jnp
from jax import lax
from jax.sharding import PartitionSpec as P

epsilon = 1e-05


def entering_2(value, axis, combine, identity, reverse):
    peers, place = (lax.axis_size(axis), lax.axis_index(axis))
    everything = jax.tree.map(lambda part: lax.all_gather(part, axis), value)
    start = jax.tree.map(
        lambda part, zero: jnp.broadcast_to(jnp.asarray(zero, part.dtype), part.shape),
        value,
        identity,
    )

    def hop(k, before):
        at = peers - 1 - k if reverse else k
        reached = at > place if reverse else at < place
        new = combine(before, jax.tree.map(lambda part: part[at], everything))
        return jax.tree.map(lambda a, b: jnp.where(reached, a, b), new, before)

    return lax.fori_loop(0, peers, hop, start)


def local_block(queries, keys_in, values_in, rates):
    length = queries.shape[0]
    cumulative = jnp.cumsum(rates, axis=0)
    scores = jnp.einsum("thd,shd->hts", queries, keys_in, preferred_element_type=jnp.float32)
    ordered = jnp.transpose(cumulative)
    spread = ordered[:, None, :] - ordered[:, :, None]
    causal = (
        lax.broadcasted_iota(jnp.int32, (length, length), 0)
        >= lax.broadcasted_iota(jnp.int32, (length, length), 1)
    )[None]
    weights = jnp.where(causal, scores * jnp.exp(jnp.where(causal, spread, 0.0)), 0.0).astype(
        jnp.bfloat16
    )
    intra_part = jnp.einsum("hts,shd->thd", weights, values_in, preferred_element_type=jnp.float32)
    return (intra_part, cumulative)


def carried(queries, cumulative, state_full):
    inter_part = jnp.einsum(
        "thd,hde->the", queries.astype(jnp.float32), state_full, precision=lax.Precision.HIGHEST
    )
    return inter_part * jnp.exp(-cumulative)[:, :, None]


def block_state(keys_in, values_in, cumulative):
    closing = cumulative[-1]
    scaled_key = (
        keys_in.astype(jnp.float32) * jnp.exp(cumulative - closing[None, :])[:, :, None]
    ).astype(jnp.bfloat16)
    state = jnp.einsum("shd,she->hde", scaled_key, values_in, preferred_element_type=jnp.float32)
    return (state, jnp.exp(-closing))


def chain_step(earlier, later):
    return (earlier[0] * later[0], later[0][:, None, None] * earlier[1] + later[1])


def multiply(earlier, later):
    return earlier * later


def local(
    document_query,
    document_key,
    document_value,
    document_decay,
    passage_query,
    passage_key,
    passage_value,
    passage_gate,
    passage_decay,
    passage_length,
    norm_gain,
):
    heads_here = document_decay.shape[1]
    head_dim = document_query.shape[1] // heads_here
    doc_rows = document_query.shape[0]
    passage_count = passage_query.shape[0]
    passage_rows = passage_query.shape[1]
    doc_queries = document_query.reshape(doc_rows, heads_here, head_dim)
    doc_keys = document_key.reshape(doc_rows, heads_here, head_dim)
    doc_values = document_value.reshape(doc_rows, heads_here, head_dim)
    intra_doc, cumulative = local_block(doc_queries, doc_keys, doc_values, document_decay)
    state_own, decay_own = block_state(doc_keys, doc_values, cumulative)
    decay_before, entering = entering_2(
        (decay_own, state_own),
        ("seq", "rep"),
        chain_step,
        (jnp.ones_like(decay_own), jnp.zeros_like(state_own)),
        False,
    )
    document_output = (intra_doc + carried(doc_queries, cumulative, entering)).astype(jnp.bfloat16)
    document_output = document_output.reshape(doc_rows, heads_here * head_dim)
    decay_after = entering_2(decay_own, ("seq", "rep"), multiply, jnp.ones_like(decay_own), True)
    memory = lax.psum(decay_after[:, None, None] * state_own, ("seq", "rep"))

    def readout(inputs):
        queries, keys_in, values_in, rates = inputs
        queries = queries.reshape(passage_rows, heads_here, head_dim)
        intra_part, running = local_block(
            queries,
            keys_in.reshape(passage_rows, heads_here, head_dim),
            values_in.reshape(passage_rows, heads_here, head_dim),
            rates,
        )
        attended = (intra_part + carried(queries, running, memory)).reshape(
            passage_rows, heads_here * head_dim
        )
        return (attended, jnp.sum(attended * attended, axis=1))

    attended, squares = lax.map(readout, (passage_query, passage_key, passage_value, passage_decay))
    totals = lax.psum(squares, "head")
    features_all = attended.shape[-1] * lax.axis_size("head")
    scaling = lax.rsqrt(totals / features_all + epsilon)
    normed = (
        attended
        * scaling[:, :, None]
        * norm_gain[None, None, :]
        * jax.nn.sigmoid(passage_gate.astype(jnp.float32))
    )
    inside = (
        lax.broadcasted_iota(jnp.int32, (passage_count, passage_rows), 1) < passage_length[:, None]
    )
    passage_output = jnp.where(inside[:, :, None], normed, 0.0).astype(jnp.bfloat16)
    return (document_output, passage_output)


def solution(mesh):
    in_specs = (
        P(("groups", "seq", "rep"), "head"),
        P(("groups", "seq", "rep"), "head"),
        P(("groups", "seq", "rep"), "head"),
        P(("groups", "seq", "rep"), "head"),
        P(("groups", "seq", "rep"), None, "head"),
        P(("groups", "seq", "rep"), None, "head"),
        P(("groups", "seq", "rep"), None, "head"),
        P(("groups", "seq", "rep"), None, "head"),
        P(("groups", "seq", "rep"), None, "head"),
        P(("groups", "seq", "rep")),
        P("head"),
    )
    out_specs = (P(("groups", "seq", "rep"), "head"), P(("groups", "seq", "rep"), None, "head"))
    return jax.shard_map(local, mesh=mesh, in_specs=in_specs, out_specs=out_specs, check_vma=False)
```

profile of v0, /device:TPU:0, one launch (start us, length us, event | category | flops | bytes accessed | tf_op | source)
XLA Modules:
  0.0 281.8 jit_solution(3076644146216741903)
XLA Ops:
  7.2 0.9 copy_bitcast_fusion.3
  8.1 0.6 reduce-window.14
  8.7 0.2 slice_reduce_fusion.1
  9.0 0.2 slice_reduce_fusion.2
  9.3 13.5 %all-gather.1 = f32[8,1,32]{2,1,0:T(1,128)S(1)} all-gather(f32[1,1,32]{2,1,0:T(1,128)S(1)} %bitcast.131), channel_id=1, replica_groups=mesh['groups'=2,'seq'=4,'head'=2,'rep'=2] {'seq','rep'}, dimensions={0}, use_global_device_ids=true | all-gather | bytes 1152 | tf_op jit(solution)/shard_map/all_gather | solution.py:11
  22.8 0.3 while.36
  23.1 4.1 %copy.82 = bf16[256,4096]{0,1:T(8,128)(2,1)} copy(bf16[256,4096]{1,0:T(8,128)(2,1)} %param.16) | data formatting | bytes 4194304 | tf_op jit(solution)/shard_map/reshape | solution.py:87
  27.1 4.4 %broadcast_multiply_fusion = (f32[32,128,128]{2,1,0:T(8,128)}, f32[32,128,128]{2,1,0:T(8,128)}) fusion(f32[32]{0:T(128)S(1)} %get-tuple-element.231, bf16[256,32,128]{0,2,1:T(8,128)(2,1)} %bitcast.121, f32[256,32]{0,1:T(8,128)S(1)} %get-tuple-element.294, bf16[256,4096]{1,0:T(8,128)(2,1)S(1)} %copy-done), kind=kOutput, calls=%fused_computation.40 | convolution fusion | flops 272105472 | bytes 8421504 | tf_op jit(solution)/shard_map/shd,she->hde/dot_general | solution.py:56
  31.6 0.7 all-gather.4.cloned.1.call-update
  32.3 0.6 reduce-window.16
  33.1 3.4 %copy.89 = bf16[32,8,32,128]{3,2,1,0:T(8,128)(2,1)} copy(bf16[32,8,32,128]{3,1,2,0:T(8,128)(2,1)} %bitcast.124) | data formatting | bytes 4194304
  36.5 4.1 %copy.81 = bf16[1,256,4096]{1,2,0:T(8,128)(2,1)} copy(bf16[1,256,4096]{2,1,0:T(8,128)(2,1)} %param.21) | data formatting | bytes 4194304 | tf_op jit(solution)/shard_map/while/body/eval_jaxpr/reshape | solution.py:109
  40.6 3.5 %copy.90 = bf16[32,8,32,128]{3,2,1,0:T(8,128)(2,1)} copy(bf16[32,8,32,128]{3,1,2,0:T(8,128)(2,1)} %bitcast.125) | data formatting | bytes 4194304
  45.0 6.4 %fusion.1 = f32[32,256,128]{1,2,0:T(8,128)} fusion(f32[32,256]{1,0:T(8,128)S(1)} %get-tuple-element.296, pred[256,256]{1,0:T(8,128)(4,1)S(1)} %iota_compare_fusion, bf16[256,32,128]{0,2,1:T(8,128)(2,1)} %bitcast.122, bf16[256,4096]{1,0:T(8,128)(2,1)S(1)} %copy-done, bf16[256,4096]{1,0:T(8,128)(2,1)} %param.15), kind=kOutput, calls=%fused_computation.7 | convolution fusion | flops 1084227584 | bytes 10584064 | tf_op jit(solution)/shard_map/hts,shd->thd/dot_general | solution.py:40
  51.3 7.3 %fusion.2 = f32[32,256,128]{1,2,0:T(8,128)} fusion(bf16[256,32,128]{0,2,1:T(8,128)(2,1)} %bitcast.126, f32[32,256]{1,0:T(8,128)S(1)} %copy_bitcast_fusion, pred[256,256]{1,0:T(8,128)(4,1)S(1)} %iota_compare_fusion, bf16[256,32,128]{2,1,0:T(8,128)(2,1)} %bitcast.127, bf16[256,32,128]{2,1,0:T(8,128)(2,1)} %bitcast.118), kind=kOutput, calls=%fused_computation.8 | convolution fusion | flops 1084227584 | bytes 10584064 | tf_op jit(solution)/shard_map/while/body/eval_jaxpr/hts,shd->thd/dot_general | solution.py:40
  58.7 36.5 %all-reduce.2.cloned.1.call-done = f32[32,128,128]{2,1,0:T(8,128)} async-done(((f32[32,128,128]{2,1,0:T(8,128)}), f32[32,128,128]{2,1,0:T(8,128)}) %all-reduce.2.cloned.1.call-update) | async-done | bytes 2097168 | tf_op jit(solution)/shard_map/psum | solution.py:101
  95.1 7.8 %multiply_reduce_fusion = (f32[256]{0:T(256)S(1)}, f32[256,32,128]{0,2,1:T(8,128)}) fusion(f32[256,32]{0,1:T(8,128)S(1)} %exponential_bitcast_fusion, f32[32,128,128]{2,1,0:T(8,128)} %all-reduce.2.cloned.1.call-done, bf16[256,32,128]{2,1,0:T(8,128)(2,1)S(1)} %bitcast.119, f32[32,256,128]{1,2,0:T(8,128)} %fusion.2), kind=kOutput, calls=%fused_computation.15 | convolution fusion | flops 1614806784 | bytes 12616704 | tf_op jit(solution)/shard_map/while/body/eval_jaxpr/thd,hde->the/dot_general | solution.py:45
  102.9 6.1 %copy.77 = f32[1,256,4096]{2,1,0:T(8,128)} copy(f32[1,256,4096]{1,2,0:T(8,128)} %bitcast.117) | data formatting | bytes 8388608 | tf_op jit(solution)/shard_map/while/body/jit(dynamic_update_index_in_dim)/broadcast_in_dim | solution.py:117
  108.9 5.1 %psum.15 = f32[1,256]{1,0:T(1,128)S(1)} all-reduce(f32[1,256]{1,0:T(1,128)S(1)} %bitcast.129), channel_id=1, replica_groups=mesh['groups'=2,'seq'=4,'head'=2,'rep'=2] {'head'}, use_global_device_ids=true, to_apply=%region_10.11 | all-reduce | flops 256 | bytes 2048 | tf_op jit(solution)/shard_map/psum | solution.py:118
  114.0 5.9 %select_convert_fusion.4 = bf16[1,256,4096]{2,1,0:T(8,128)(2,1)} fusion(bf16[1,256,4096]{2,1,0:T(8,128)(2,1)} %param.22, f32[1,256,4096]{2,1,0:T(8,128)} %copy.77, f32[4096]{0:T(1024)S(1)} %copy-done.5, f32[256]{0:T(256)S(1)} %bitcast.130, pred[256]{0:T(512)(128)(4,1)S(1)} %iota_compare_fusion.1), kind=kLoop, calls=%fused_computation.14 | loop fusion | flops 9437184 | bytes 8406272 | tf_op jit(solution)/shard_map/convert_element_type | solution.py:130
  119.9 127.5 %all-gather.4.cloned.1.call-done = f32[256,128,128]{2,1,0:T(8,128)} async-done(((f32[32,128,128]{2,1,0:T(8,128)}), f32[256,128,128]{2,1,0:T(8,128)}) %all-gather.4.cloned.1.call-update) | async-done | bytes 16777232 | tf_op jit(solution)/shard_map/all_gather | solution.py:11
  247.4 17.0 %while.35 = (s32[]{:T(128)}, f32[32,128,128]{2,1,0:T(8,128)S(1)}, s32[]{:T(128)}, f32[8,32]{1,0:T(8,128)S(1)}, f32[8,32,128,128]{3,2,1,0:T(8,128)}, /*index=5*/s32[]{:T(128)}, s32[]{:T(128)}) while((s32[]{:T(128)}, f32[32,128,128]{2,1,0:T(8,128)S(1)}, s32[]{:T(128)}, f32[8,32]{1,0:T(8,128)S(1)}, f32[8,32,128,128]{3,2,1,0:T(8,128)}, ...), condition=%wide.region_3.4_spmd.clone, body=%wide.region_2.3_spmd.clone.sunk | while | flops 2097156 | bytes 6291945 | solution.py:24
  247.4 2.1 fusion.49
  249.6 2.1 fusion.49
  251.7 2.1 fusion.49
  253.8 2.1 fusion.49
  256.0 2.1 fusion.49
  258.1 2.1 fusion.49
  260.2 2.1 fusion.49
  262.4 2.1 fusion.49
  264.5 6.3 %fusion.5 = bf16[256,32,128]{0,2,1:T(8,128)(2,1)} fusion(f32[32,256,128]{1,2,0:T(8,128)} %fusion.1, f32[32,128,128]{2,1,0:T(8,128)S(1)} %get-tuple-element.230, f32[256,32]{0,1:T(8,128)S(1)} %get-tuple-element.293, bf16[256,4096]{1,0:T(8,128)(2,1)} %param.15), kind=kOutput, calls=%fused_computation.13 | convolution fusion | flops 1613758464 | bytes 10518528 | tf_op jit(solution)/shard_map/thd,hde->the/dot_general | solution.py:45
  270.8 4.2 %copy.78 = bf16[256,4096]{1,0:T(8,128)(2,1)} copy(bf16[256,4096]{0,1:T(8,128)(2,1)} %bitcast.120) | data formatting | bytes 4194304
  (46 shorter events, 0.9 us)
Async XLA Ops:
  7.2 20.0 %copy-start = (bf16[256,4096]{1,0:T(8,128)(2,1)S(1)}, bf16[256,4096]{1,0:T(8,128)(2,1)}, u32[]{:S(2)}) copy-start(bf16[256,4096]{1,0:T(8,128)(2,1)} %param.17) | copy-start | bytes 6291460
  7.2 87.9 %all-reduce.2.cloned.1.call-start = ((), (), s32[]{:S(2)}) async-start(), calls=%async_computation | async-start | bytes 4194304 | tf_op jit(solution)/shard_map/psum | solution.py:101
  31.5 0.8 copy-start.4
  31.6 215.9 %all-gather.4.cloned.1.call-start = ((), (), s32[]{:S(2)}) async-start(), calls=%async_computation.1 | async-start | bytes 18874368 | tf_op jit(solution)/shard_map/all_gather | solution.py:11
  51.3 43.8 %copy-start.3 = (bf16[32,8,32,128]{3,2,1,0:T(8,128)(2,1)S(1)}, bf16[32,8,32,128]{3,2,1,0:T(8,128)(2,1)}, u32[]{:S(2)}) copy-start(bf16[32,8,32,128]{3,2,1,0:T(8,128)(2,1)} %copy.89) | copy-start | bytes 6291460
  102.9 11.2 %copy-start.5 = (f32[4096]{0:T(1024)S(1)}, f32[4096]{0:T(1024)}, u32[]{:S(2)}) copy-start(f32[4096]{0:T(1024)} %param.25) | copy-start | bytes 49156
  114.0 133.4 %copy-start.2 = (f32[32,128,128]{2,1,0:T(8,128)S(1)}, f32[32,128,128]{2,1,0:T(8,128)}, u32[]{:S(2)}) copy-start(f32[32,128,128]{2,1,0:T(8,128)} %custom-call) | copy-start | bytes 6291460
  270.8 4.2 %copy-start.1 = (bf16[256,4096]{1,0:T(8,128)(2,1)S(1)}, bf16[256,4096]{1,0:T(8,128)(2,1)}, u32[]{:S(2)}) copy-start(bf16[256,4096]{1,0:T(8,128)(2,1)} %param.17) | copy-start | bytes 6291460
Sparse Core Ops, SparseCore 0:
  31.7 63.3 all-reduce.1
  96.7 150.6 all-gather.3
where the time goes:
time: 283 us; the launch traced here: 282 us
  waiting for transfers between devices  165 us (58%)
  matrix products  32.1 us (11%)
  local copies, waits for them, and re-layouts  26.6 us (9%)
  other arithmetic  24.6 us (9%)
  blocking collectives  18.6 us (7%)
  between operations  14.8 us (5%)
    all_gather x1, waiting for transfers between devices, entering_2(): everything = jax.tree.map(lambda part: lax.all_gather(part, axis), value)  128 us
    psum x1, waiting for transfers between devices, local(): memory = lax.psum(decay_after[:, None, None] * state_own, ('seq', 'rep'))  36.5 us
    select_n x16, other arithmetic, hop(): return jax.tree.map(lambda a, b: jnp.where(reached, a, b), new, before)  16.9 us
    dot_general x2, matrix products, carried(): jnp.einsum('thd,hde->the', queries.astype(jnp.float32), state_full, preci...  14 us
    dot_general x2, matrix products, local_block(): jnp.einsum('hts,shd->thd', weights, values_in, preferred_element_type=jnp...  13.7 us
    all_gather x1, blocking collectives, entering_2(): everything = jax.tree.map(lambda part: lax.all_gather(part, axis), value)  13.5 us
    unnamed x15, local copies, waits for them, and re-layouts  11.1 us
    broadcast_in_dim x1, local copies, waits for them, and re-layouts, local(): lax.map(readout, (passage_query, passage_key, passage_value, passage_decay))  6.07 us
  transfers between devices with their start and end apart: 2, of which 2 were waited for; matrix products, arithmetic and copies ran while one was open for 16% of the time, Pallas kernels for 0%

commit v1 on v0

--- a/solution.py
+++ b/solution.py
@@ -98,7 +98,9 @@
     document_output = (intra_doc + carried(doc_queries, cumulative, entering)).astype(jnp.bfloat16)
     document_output = document_output.reshape(doc_rows, heads_here * head_dim)
     decay_after = entering_2(decay_own, ("seq", "rep"), multiply, jnp.ones_like(decay_own), True)
-    memory = lax.psum(decay_after[:, None, None] * state_own, ("seq", "rep"))
+    own = decay_after[:, None, None] * state_own
+    parts = lax.all_gather(own, ("seq", "rep"), axis=0, tiled=False)
+    memory = parts.sum(axis=0)
 
     def readout(inputs):
         queries, keys_in, values_in, rates = inputs

time: 283 us -> 373 us (1.32)
  waiting for transfers between devices: 165 us -> 244 us
  other arithmetic: 24.6 us -> 33.7 us
    all_gather x0 -> x1, waiting for transfers between devices: none -> 122 us  [local(): parts = lax.all_gather(own, ('seq', 'rep'), axis=0, tiled=False)]
    psum x1 -> x0, waiting for transfers between devices: 36.5 us -> none  [local(): memory = lax.psum(decay_after[:, None, None] * state_own, ('seq', 'rep'))]
    reduce_sum x0 -> x1, other arithmetic: none -> 9.21 us  [local(): memory = parts.sum(axis=0)]
    all_gather x1, waiting for transfers between devices: 128 us -> 122 us  [entering_2(): everything = jax.tree.map(lambda part: lax.all_gather(part, axis), value)]
  transfers between devices with their start and end apart: 2 -> 2, of which waited for: 2 -> 2; matrix products, arithmetic and copies ran while one was open for 16% -> 14% of each run, Pallas kernels for 0% -> 0%
where the time goes in v1:
time: 373 us; the launch traced here: 372 us
  waiting for transfers between devices  244 us (65%)
  other arithmetic  33.7 us (9%)
  matrix products  33 us (9%)
  local copies, waits for them, and re-layouts  27.1 us (7%)
  blocking collectives  18.6 us (5%)
  between operations  14.8 us (4%)
    all_gather x1, waiting for transfers between devices, local(): parts = lax.all_gather(own, ('seq', 'rep'), axis=0, tiled=False)  122 us
    all_gather x1, waiting for transfers between devices, entering_2(): everything = jax.tree.map(lambda part: lax.all_gather(part, axis), value)  122 us
    select_n x16, other arithmetic, hop(): return jax.tree.map(lambda a, b: jnp.where(reached, a, b), new, before)  16.9 us
    dot_general x2, matrix products, carried(): jnp.einsum('thd,hde->the', queries.astype(jnp.float32), state_full, preci...  15.2 us
    dot_general x2, matrix products, local_block(): jnp.einsum('hts,shd->thd', weights, values_in, preferred_element_type=jnp...  13.5 us
    all_gather x1, blocking collectives, entering_2(): everything = jax.tree.map(lambda part: lax.all_gather(part, axis), value)  13.5 us
    unnamed x15, local copies, waits for them, and re-layouts  11.5 us
    reduce_sum x1, other arithmetic, local(): memory = parts.sum(axis=0)  9.21 us
  transfers between devices with their start and end apart: 2, of which 2 were waited for; matrix products, arithmetic and copies ran while one was open for 14% of the time, Pallas kernels for 0%

profile of v1, /device:TPU:0, one launch (start us, length us, event | category | flops | bytes accessed | tf_op | source)
XLA Modules:
  0.0 371.8 jit_solution(14747369189208727173)
XLA Ops:
  7.2 0.9 copy_bitcast_fusion.3
  8.1 0.6 reduce-window.14
  9.0 0.2 slice_reduce_fusion.2
  9.3 13.5 %all-gather.2 = f32[8,1,32]{2,1,0:T(1,128)S(1)} all-gather(f32[1,1,32]{2,1,0:T(1,128)S(1)} %bitcast.133), channel_id=1, replica_groups=mesh['groups'=2,'seq'=4,'head'=2,'rep'=2] {'seq','rep'}, dimensions={0}, use_global_device_ids=true | all-gather | bytes 1152 | tf_op jit(solution)/shard_map/all_gather | solution.py:11
  22.8 0.3 while.36
  23.1 4.1 %copy.79 = bf16[256,4096]{0,1:T(8,128)(2,1)} copy(bf16[256,4096]{1,0:T(8,128)(2,1)} %param.16) | data formatting | bytes 4194304 | tf_op jit(solution)/shard_map/reshape | solution.py:87
  27.1 4.3 %broadcast_multiply_fusion = (f32[32,128,128]{2,1,0:T(8,128)}, f32[32,128,128]{2,1,0:T(8,128)}) fusion(f32[32]{0:T(128)S(1)} %get-tuple-element.231, bf16[256,32,128]{0,2,1:T(8,128)(2,1)} %bitcast.123, f32[256,32]{0,1:T(8,128)S(1)} %get-tuple-element.294, bf16[256,4096]{1,0:T(8,128)(2,1)S(1)} %copy-done), kind=kOutput, calls=%fused_computation.40 | convolution fusion | flops 272105472 | bytes 8421504 | tf_op jit(solution)/shard_map/shd,she->hde/dot_general | solution.py:56
  31.5 0.7 all-gather.6.cloned.1.call-update
  32.2 0.6 reduce-window.16
  33.0 3.4 copy.86
  36.5 4.3 %copy.78 = bf16[1,256,4096]{1,2,0:T(8,128)(2,1)} copy(bf16[1,256,4096]{2,1,0:T(8,128)(2,1)} %param.21) | data formatting | bytes 4194304 | tf_op jit(solution)/shard_map/while/body/eval_jaxpr/reshape | solution.py:111
  40.7 4.0 %copy.87 = bf16[32,8,32,128]{3,2,1,0:T(8,128)(2,1)} copy(bf16[32,8,32,128]{3,1,2,0:T(8,128)(2,1)} %bitcast.127) | data formatting | bytes 4194304
  45.6 6.4 %fusion.1 = f32[32,256,128]{1,2,0:T(8,128)} fusion(f32[32,256]{1,0:T(8,128)S(1)} %get-tuple-element.296, pred[256,256]{1,0:T(8,128)(4,1)S(1)} %iota_compare_fusion, bf16[256,32,128]{0,2,1:T(8,128)(2,1)} %bitcast.124, bf16[256,4096]{1,0:T(8,128)(2,1)S(1)} %copy-done, bf16[256,4096]{1,0:T(8,128)(2,1)} %param.15), kind=kOutput, calls=%fused_computation.7 | convolution fusion | flops 1084227584 | bytes 10584064 | tf_op jit(solution)/shard_map/hts,shd->thd/dot_general | solution.py:40
  52.0 7.1 %fusion.2 = f32[32,256,128]{1,2,0:T(8,128)} fusion(bf16[256,32,128]{0,2,1:T(8,128)(2,1)} %bitcast.128, f32[32,256]{1,0:T(8,128)S(1)} %copy_bitcast_fusion, pred[256,256]{1,0:T(8,128)(4,1)S(1)} %iota_compare_fusion, bf16[256,32,128]{2,1,0:T(8,128)(2,1)} %bitcast.129, bf16[256,32,128]{2,1,0:T(8,128)(2,1)} %bitcast.120), kind=kOutput, calls=%fused_computation.8 | convolution fusion | flops 1084227584 | bytes 10584064 | tf_op jit(solution)/shard_map/while/body/eval_jaxpr/hts,shd->thd/dot_general | solution.py:40
  59.1 121.8 %all-gather.8.cloned.1.call-done = f32[256,128,128]{2,1,0:T(8,128)} async-done(((f32[32,128,128]{2,1,0:T(8,128)}), f32[256,128,128]{2,1,0:T(8,128)}) %all-gather.8.cloned.1.call-update) | async-done | bytes 16777232 | tf_op jit(solution)/shard_map/all_gather | solution.py:102
  180.9 9.2 %reduce_sum.19 = f32[32,128,128]{2,1,0:T(8,128)} reduce(f32[8,32,128,128]{3,2,1,0:T(8,128)} %bitcast.119, f32[]{:T(128)} %constant.101.clone.1), dimensions={0}, to_apply=%region_8.9 | reduce | flops 3670016 | bytes 18874372 | tf_op jit(solution)/shard_map/reduce_sum | solution.py:103
  190.1 9.0 %multiply_reduce_fusion = (f32[256]{0:T(256)S(1)}, f32[256,32,128]{0,2,1:T(8,128)}) fusion(f32[256,32]{0,1:T(8,128)S(1)} %exponential_bitcast_fusion, f32[32,128,128]{2,1,0:T(8,128)} %reduce_sum.19, bf16[256,32,128]{2,1,0:T(8,128)(2,1)S(1)} %bitcast.121, f32[32,256,128]{1,2,0:T(8,128)} %fusion.2), kind=kOutput, calls=%fused_computation.15 | convolution fusion | flops 1614806784 | bytes 12616704 | tf_op jit(solution)/shard_map/while/body/eval_jaxpr/thd,hde->the/dot_general | solution.py:45
  199.1 5.9 %copy.74 = f32[1,256,4096]{2,1,0:T(8,128)} copy(f32[1,256,4096]{1,2,0:T(8,128)} %bitcast.118) | data formatting | bytes 8388608 | tf_op jit(solution)/shard_map/while/body/jit(dynamic_update_index_in_dim)/broadcast_in_dim | solution.py:119
  205.0 5.1 %psum.7 = f32[1,256]{1,0:T(1,128)S(1)} all-reduce(f32[1,256]{1,0:T(1,128)S(1)} %bitcast.132), channel_id=1, replica_groups=mesh['groups'=2,'seq'=4,'head'=2,'rep'=2] {'head'}, use_global_device_ids=true, to_apply=%region_10.11 | all-reduce | flops 256 | bytes 2048 | tf_op jit(solution)/shard_map/psum | solution.py:120
  210.1 121.7 %all-gather.6.cloned.1.call-done = f32[256,128,128]{2,1,0:T(8,128)} async-done(((f32[32,128,128]{2,1,0:T(8,128)}), f32[256,128,128]{2,1,0:T(8,128)}) %all-gather.6.cloned.1.call-update) | async-done | bytes 16777232 | tf_op jit(solution)/shard_map/all_gather | solution.py:11
  331.8 17.0 %while.35 = (s32[]{:T(128)}, f32[32,128,128]{2,1,0:T(8,128)S(1)}, s32[]{:T(128)}, f32[8,32]{1,0:T(8,128)S(1)}, f32[8,32,128,128]{3,2,1,0:T(8,128)}, /*index=5*/s32[]{:T(128)}, s32[]{:T(128)}) while((s32[]{:T(128)}, f32[32,128,128]{2,1,0:T(8,128)S(1)}, s32[]{:T(128)}, f32[8,32]{1,0:T(8,128)S(1)}, f32[8,32,128,128]{3,2,1,0:T(8,128)}, ...), condition=%wide.region_3.4_spmd.clone, body=%wide.region_2.3_spmd.clone.sunk | while | flops 2097156 | bytes 6291945 | solution.py:24
  331.8 2.1 fusion.49
  334.0 2.1 fusion.49
  336.1 2.1 fusion.49
  338.2 2.1 fusion.49
  340.4 2.1 fusion.49
  342.5 2.1 fusion.49
  344.6 2.1 fusion.49
  346.8 2.1 fusion.49
  348.9 6.3 %fusion.5 = bf16[256,32,128]{0,2,1:T(8,128)(2,1)} fusion(f32[32,256,128]{1,2,0:T(8,128)} %fusion.1, f32[32,128,128]{2,1,0:T(8,128)S(1)} %get-tuple-element.230, f32[256,32]{0,1:T(8,128)S(1)} %get-tuple-element.293, bf16[256,4096]{1,0:T(8,128)(2,1)} %param.15), kind=kOutput, calls=%fused_computation.13 | convolution fusion | flops 1613758464 | bytes 10518528 | tf_op jit(solution)/shard_map/thd,hde->the/dot_general | solution.py:45
  355.1 4.1 %copy.75 = bf16[256,4096]{1,0:T(8,128)(2,1)} copy(bf16[256,4096]{0,1:T(8,128)(2,1)} %bitcast.122) | data formatting | bytes 4194304
  359.2 5.8 %select_convert_fusion.4 = bf16[1,256,4096]{2,1,0:T(8,128)(2,1)} fusion(bf16[1,256,4096]{2,1,0:T(8,128)(2,1)} %param.22, f32[1,256,4096]{2,1,0:T(8,128)} %copy.74, f32[4096]{0:T(1024)S(1)} %copy-done.5, f32[256]{0:T(256)S(1)} %bitcast.131, pred[256]{0:T(512)(128)(4,1)S(1)} %iota_compare_fusion.1), kind=kLoop, calls=%fused_computation.14 | loop fusion | flops 9437184 | bytes 8406272 | tf_op jit(solution)/shard_map/convert_element_type | solution.py:132
  (47 shorter events, 1.1 us)
Async XLA Ops:
  7.2 20.0 %copy-start = (bf16[256,4096]{1,0:T(8,128)(2,1)S(1)}, bf16[256,4096]{1,0:T(8,128)(2,1)}, u32[]{:S(2)}) copy-start(bf16[256,4096]{1,0:T(8,128)(2,1)} %param.17) | copy-start | bytes 6291460
  7.2 173.7 %all-gather.8.cloned.1.call-start = ((), (), s32[]{:S(2)}) async-start(), calls=%async_computation.1 | async-start | bytes 18874368 | tf_op jit(solution)/shard_map/all_gather | solution.py:102
  31.4 0.8 copy-start.4
  31.4 300.4 %all-gather.6.cloned.1.call-start = ((), (), s32[]{:S(2)}) async-start(), calls=%async_computation | async-start | bytes 18874368 | tf_op jit(solution)/shard_map/all_gather | solution.py:11
  180.9 9.2 %copy-start.3 = (bf16[32,8,32,128]{3,2,1,0:T(8,128)(2,1)S(1)}, bf16[32,8,32,128]{3,2,1,0:T(8,128)(2,1)}, u32[]{:S(2)}) copy-start(bf16[32,8,32,128]{3,2,1,0:T(8,128)(2,1)} %copy.86) | copy-start | bytes 6291460
  199.1 132.7 %copy-start.2 = (f32[32,128,128]{2,1,0:T(8,128)S(1)}, f32[32,128,128]{2,1,0:T(8,128)}, u32[]{:S(2)}) copy-start(f32[32,128,128]{2,1,0:T(8,128)} %custom-call) | copy-start | bytes 6291460
  355.1 4.1 %copy-start.5 = (f32[4096]{0:T(1024)S(1)}, f32[4096]{0:T(1024)}, u32[]{:S(2)}) copy-start(f32[4096]{0:T(1024)} %param.25) | copy-start | bytes 49156
  359.2 5.8 %copy-start.1 = (bf16[256,4096]{1,0:T(8,128)(2,1)S(1)}, bf16[256,4096]{1,0:T(8,128)(2,1)}, u32[]{:S(2)}) copy-start(bf16[256,4096]{1,0:T(8,128)(2,1)} %param.17) | copy-start | bytes 6291460
Sparse Core Ops, SparseCore 0:
  31.6 149.3 all-gather.7
  182.5 149.2 all-gather.5
